TPU v7x, 256 devices: a whole 4x4x8 slice. The times are simulated.
256 devices in a mesh: cell: 32 (over y_hi, z, core), brick: 8 (over x, y_lo).
Axes of the slice: x: 4, y: 4 (y_hi: 2, y_lo: 2; y = y_hi * 2 + y_lo), z: 8, core: 2. Of those that a mesh axis runs over, the one named last changes fastest.
Arguments:
- features: bfloat16 [32, 8, 128, 256], P('cell', 'brick'), may hold values from -6 to 6
- species: int32 [32, 8, 128], P('cell', 'brick'), may hold values from 0 to 3
- species_table: bfloat16 [4, 256], replicated, may hold values from -3 to 3
- neighbours: int32 [32, 8, 64, 128], P('cell', 'brick'), may hold values from 0 to 383
- counts: int32 [32, 8, 128], P('cell', 'brick'), may hold values from 1 to 64
- send_lists: int32 [32, 8, 8, 32], P('cell', 'brick'), may hold values from 0 to 127
- distances: float32 [32, 8, 64, 128], P('cell', 'brick'), may hold values from 0.05 to 1
- head_decay: float32 [8], replicated, may hold values from 0.25 to 4
- norm_gain: float32 [256], replicated, may hold values from 0.5 to 1.5
- readout: float32 [256], replicated, may hold values from -0.375 to 0.375
- targets: float32 [32, 8, 128], P('cell', 'brick'), may hold values from -6 to 6
- master: float32 [4, 256, 256], P(None, 'cell'), as said below
- moment: float32 [4, 256, 256], P(None, 'cell'), may hold values from -3 to 3
- second: float32 [4, 256, 256], P(None, 'cell'), may hold values from 0.1 to 1
Outputs:
- energies: float32 [32, 8, 128], P('cell', 'brick')
- moment_new: float32 [4, 256, 256], P(None, 'cell')
- second_new: float32 [4, 256, 256], P(None, 'cell')
- adam_step: float32 [4, 256, 256], P(None, 'cell')
Inputs may be any that keep to these rules, and one draw needn't show every extreme that they name: `master`: projection entries lie within -48 * 256^-0.5 and 48 * 256^-0.5.
All inputs are finite; a program needn't handle non-finite values.
Results may differ from a plain program's by a relative error of at most 0.0045.
The roundings to bfloat16 on the way count: a program that leaves them out, or rounds other values in their place, can miss the bound.
Values may be sent and summed in bfloat16 or wider, within the bound.
A program may use at most 64 MiB of HBM per device.

v0:
```python
import math
import jax
import jax.numpy as jnp
from jax import lax
from jax.sharding import PartitionSpec as P

TILE = 128
loss_weight = 0.0625
epsilon_norm = 1e-06


def silu_slope(inputs):
    sigmoid_val = jax.nn.sigmoid(inputs)
    return sigmoid_val * (1.0 + inputs * (1.0 - sigmoid_val))


def normalize(embedded, norm_gain):
    rms_scale = lax.rsqrt(jnp.mean(embedded * embedded, axis=-1, keepdims=True) + epsilon_norm)
    return (embedded * rms_scale * norm_gain).astype(jnp.bfloat16)


def brick_sweep(
    query,
    key_table,
    value_table,
    embedded,
    neighbour_rows,
    local_count,
    local_dist,
    local_target,
    out_proj,
    head_decay,
    readout,
):
    atom_count, model_width = query.shape
    head_count = head_decay.shape[0]
    head_size = model_width // head_count
    slot_count = neighbour_rows.shape[0]
    score_scale = 1.0 / math.sqrt(head_size)
    table_rows = key_table.shape[0]

    def tile_step(grad_carry, tile_index):
        key_grads, value_grads = grad_carry
        key_rows = key_table[neighbour_rows].reshape(slot_count, TILE, head_count, head_size)
        value_rows = value_table[neighbour_rows].reshape(slot_count, TILE, head_count, head_size)
        query_heads = query.reshape(TILE, head_count, head_size)
        is_valid = (jnp.arange(slot_count)[:, None] < local_count[None, :])[:, :, None]
        score = (
            jnp.einsum("ahd,kahd->kah", query_heads, key_rows, preferred_element_type=jnp.float32)
            * score_scale
        )
        score = score - head_decay[None, None, :] * local_dist[:, :, None]
        score = jnp.where(is_valid, score, -1e30)
        row_max = jnp.max(score, axis=0, keepdims=True)
        exp_terms = jnp.where(is_valid, jnp.exp(score - row_max), 0.0)
        attention = exp_terms / jnp.sum(exp_terms, axis=0, keepdims=True)
        attention_half = attention.astype(jnp.bfloat16)
        attended = jnp.einsum(
            "kah,kahd->ahd", attention_half, value_rows, preferred_element_type=jnp.float32
        )
        attended = attended.astype(jnp.bfloat16).reshape(TILE, model_width)
        updated = embedded + jnp.dot(attended, out_proj, preferred_element_type=jnp.float32)
        energy = jnp.sum(readout * jax.nn.silu(updated), axis=-1)
        grad_energy = loss_weight * (energy - local_target)
        grad_updated = (grad_energy[:, None] * readout * silu_slope(updated)).astype(jnp.bfloat16)
        grad_attended = jnp.einsum(
            "ad,cd->ac", grad_updated, out_proj, preferred_element_type=jnp.float32
        ).astype(jnp.bfloat16)
        grad_att_heads = grad_attended.reshape(TILE, head_count, head_size)
        grad_weights = jnp.einsum(
            "ahd,kahd->kah", grad_att_heads, value_rows, preferred_element_type=jnp.float32
        )
        grad_score = attention * (
            grad_weights - jnp.sum(attention * grad_weights, axis=0, keepdims=True)
        )
        grad_score = grad_score.astype(jnp.bfloat16)
        grad_query = (
            jnp.einsum("kah,kahd->ahd", grad_score, key_rows, preferred_element_type=jnp.float32)
            * score_scale
        )
        grad_query = grad_query.astype(jnp.bfloat16).reshape(TILE, model_width)
        key_edge = (
            grad_score.astype(jnp.float32)[..., None]
            * query_heads.astype(jnp.float32)[None]
            * score_scale
        )
        value_edge = (
            attention_half.astype(jnp.float32)[..., None] * grad_att_heads.astype(jnp.float32)[None]
        )
        flattened_rows = neighbour_rows.reshape(-1)
        key_grads = key_grads.at[flattened_rows].add(key_edge.reshape(-1, model_width))
        value_grads = value_grads.at[flattened_rows].add(value_edge.reshape(-1, model_width))
        return ((key_grads, value_grads), (energy, attended, grad_updated, grad_query))

    start_grads = (
        jnp.zeros((table_rows, model_width), jnp.float32),
        jnp.zeros((table_rows, model_width), jnp.float32),
    )
    (key_grads, value_grads), stacked = lax.scan(
        tile_step, start_grads, jnp.arange(atom_count // TILE, dtype=jnp.int32)
    )
    energy, attended, grad_updated, grad_query = stacked
    return (
        key_grads,
        value_grads,
        energy.reshape(atom_count),
        attended.reshape(atom_count, model_width),
        grad_updated.reshape(atom_count, model_width),
        grad_query.reshape(atom_count, model_width),
    )


def body(
    features,
    species,
    species_table,
    neighbours,
    counts,
    send_lists,
    distances,
    head_decay,
    norm_gain,
    readout,
    targets,
    master,
    moment,
    second,
):
    local_feat = features[0, 0]
    local_species = species[0, 0]
    neighbour_rows = neighbours[0, 0]
    local_count = counts[0, 0]
    send_rows = send_lists[0, 0]
    local_dist = distances[0, 0]
    local_target = targets[0, 0]
    atom_count, model_width = local_feat.shape
    bricks, ghost_position = send_rows.shape
    species_count = species_table.shape[0]
    picked = (local_species[:, None] == jnp.arange(species_count)[None, :]).astype(jnp.bfloat16)
    embedded = local_feat.astype(jnp.float32) + jnp.dot(
        picked, species_table, preferred_element_type=jnp.float32
    )
    normed_features = normalize(embedded, norm_gain)
    attention_weights = lax.all_gather(master.astype(jnp.bfloat16), "cell", axis=1, tiled=True)
    projected = jnp.einsum(
        "pe,mer->mpr", normed_features, attention_weights[0:3], preferred_element_type=jnp.float32
    ).astype(jnp.bfloat16)
    flat_send = send_rows.reshape(-1)
    parcel = projected[1:3][:, flat_send].reshape(2, bricks, ghost_position, model_width)
    arrived = lax.all_to_all(parcel, "brick", split_axis=1, concat_axis=1, tiled=True)
    ghost_keys = arrived[0].reshape(-1, model_width)
    ghost_values = arrived[1].reshape(-1, model_width)
    key_table = jnp.concatenate([projected[1], ghost_keys], axis=0)
    value_table = jnp.concatenate([projected[2], ghost_values], axis=0)
    key_grads, value_grads, energy, attended, grad_updated, grad_query = brick_sweep(
        projected[0],
        key_table,
        value_table,
        embedded,
        neighbour_rows,
        local_count,
        local_dist,
        local_target,
        attention_weights[3],
        head_decay,
        readout,
    )
    ghost_grads = jnp.stack([key_grads[atom_count:], value_grads[atom_count:]]).reshape(
        2, bricks, ghost_position, model_width
    )
    returned = lax.all_to_all(
        ghost_grads.astype(jnp.bfloat16), "brick", split_axis=1, concat_axis=1, tiled=True
    ).astype(ghost_grads.dtype)
    local_portion = jnp.stack([key_grads[:atom_count], value_grads[:atom_count]])
    totals = (
        local_portion.at[:, flat_send]
        .add(returned.reshape(2, -1, model_width))
        .astype(jnp.bfloat16)
    )
    grad_q = jnp.einsum(
        "ac,ad->cd", normed_features, grad_query, preferred_element_type=jnp.float32
    )
    key_gradient = jnp.einsum(
        "ac,ad->cd", normed_features, totals[0], preferred_element_type=jnp.float32
    )
    grad_v = jnp.einsum("ac,ad->cd", normed_features, totals[1], preferred_element_type=jnp.float32)
    grad_o = jnp.einsum("ac,ad->cd", attended, grad_updated, preferred_element_type=jnp.float32)
    grads = jnp.stack([grad_q, key_gradient, grad_v, grad_o])
    summed = lax.psum(grads.astype(jnp.bfloat16), "brick")
    owned = lax.psum_scatter(summed, "cell", scatter_dimension=1, tiled=True).astype(jnp.float32)
    moment_new = 0.9 * moment + 0.1 * owned
    second_new = 0.999 * second + 0.001 * owned * owned
    adam_step = moment_new / (jnp.sqrt(second_new) + 1e-08)
    return (energy[None, None, :], moment_new, second_new, adam_step)


def solution(mesh):
    return jax.shard_map(
        body,
        mesh=mesh,
        in_specs=(
            P("cell", "brick", None, None),
            P("cell", "brick", None),
            P(),
            P("cell", "brick", None, None),
            P("cell", "brick", None),
            P("cell", "brick", None, None),
            P("cell", "brick", None, None),
            P(),
            P(),
            P(),
            P("cell", "brick", None),
            P(None, "cell", None),
            P(None, "cell", None),
            P(None, "cell", None),
        ),
        out_specs=(
            P("cell", "brick", None),
            P(None, "cell", None),
            P(None, "cell", None),
            P(None, "cell", None),
        ),
        check_vma=False,
    )
```

profile of v0, /device:TPU:16, one launch (start us, length us, event | category | flops | bytes accessed | tf_op | source)
XLA Modules:
  0.0 491.4 jit_solution(7539827670805211175)
XLA Ops:
  7.2 0.8 reshape_squeeze.17
  8.0 0.8 convert_element_type.79
  8.7 1.2 multiply_reduce_fusion.5
  9.9 43.4 %all_gather.3 = bf16[4,256,256]{2,1,0:T(8,128)(2,1)S(1)} all-gather(bf16[4,8,256]{2,1,0:T(8,128)(2,1)S(1)} %convert_element_type.79), channel_id=1, replica_groups=mesh['cell'=32,'brick'=8] {'cell'}, dimensions={1}, use_global_device_ids=true | all-gather | bytes 540672 | tf_op jit(solution)/shard_map/all_gather | solution.py:144
  53.3 0.8 multiply_convert_fusion.2
  54.1 0.2 fusion.10
  54.5 1.2 gather_fusion
  55.7 0.7 copy.53
  56.4 5.9 %all-to-all-start = ((bf16[2,8,32,256]{3,2,0,1:T(8,128)(2,1)}), bf16[2,8,32,256]{3,2,0,1:T(8,128)(2,1)S(1)}, u32[]{:S(2)}, u32[]{:S(2)}) async-start(bf16[2,8,32,256]{3,2,0,1:T(8,128)(2,1)} %copy.53), calls=%async_computation | async-start | bytes 524288 | tf_op jit(solution)/shard_map/all_to_all | solution.py:150
  62.4 0.8 compare_select_fusion
  63.2 0.7 iota_compare_fusion.2
  64.0 0.8 fusion.37
  64.8 5.0 %all-to-all-done = bf16[2,8,32,256]{3,2,0,1:T(8,128)(2,1)S(1)} async-done(((bf16[2,8,32,256]{3,2,0,1:T(8,128)(2,1)}), bf16[2,8,32,256]{3,2,0,1:T(8,128)(2,1)S(1)}, u32[]{:S(2)}, u32[]{:S(2)}) %all-to-all-start) | async-done | bytes 262176 | tf_op jit(solution)/shard_map/all_to_all | solution.py:150
  69.9 32.9 %gather_fusion.1 = bf16[8192,256]{1,0:T(8,128)(2,1)} fusion(bf16[384,256]{1,0:T(8,128)(2,1)S(1)} %get-tuple-element.81, s32[8192]{0:T(1024)S(1)} %fusion.37), kind=kCustom, calls=%fused_computation.1 | custom fusion | bytes 8421376 | tf_op jit(solution)/shard_map/while/body/eval_jaxpr/gather | solution.py:44
  102.8 6.4 %copy.55 = bf16[8192,256]{0,1:T(8,128)(2,1)} copy(bf16[8192,256]{1,0:T(8,128)(2,1)} %gather_fusion.1) | data formatting | bytes 8388608 | tf_op jit(solution)/shard_map/while/body/eval_jaxpr/gather | solution.py:44
  109.2 5.3 %copy.103 = bf16[32,8,64,128]{3,2,1,0:T(8,128)(2,1)} copy(bf16[32,8,64,128]{3,1,2,0:T(8,128)(2,1)} %bitcast.154) | data formatting | bytes 8388608
  114.5 32.9 %gather_fusion.2 = bf16[8192,256]{1,0:T(8,128)(2,1)} fusion(bf16[384,256]{1,0:T(8,128)(2,1)S(1)} %get-tuple-element.82, s32[8192]{0:T(1024)S(1)} %fusion.37), kind=kCustom, calls=%fused_computation.2 | custom fusion | bytes 8421376 | tf_op jit(solution)/shard_map/while/body/eval_jaxpr/gather | solution.py:45
  147.4 6.7 %copy.58 = bf16[8192,256]{0,1:T(8,128)(2,1)} copy(bf16[8192,256]{1,0:T(8,128)(2,1)} %gather_fusion.2) | data formatting | bytes 8388608 | tf_op jit(solution)/shard_map/while/body/eval_jaxpr/gather | solution.py:45
  154.2 5.5 %copy.104 = bf16[32,8,64,128]{3,2,1,0:T(8,128)(2,1)} copy(bf16[32,8,64,128]{3,1,2,0:T(8,128)(2,1)} %bitcast.155) | data formatting | bytes 8388608
  159.7 1.2 multiply_reduce_fusion.3
  160.9 1.1 convert_convert_fusion
  162.0 4.0 multiply_reduce_fusion.2
  166.0 0.3 multiply_reduce_fusion.4
  166.3 0.2 convolution_convert_fusion.5
  166.7 3.4 multiply_reduce_fusion.1
  170.1 1.1 broadcast_multiply_fusion
  171.2 22.6 %copy.118 = f32[32,8,64,128]{3,1,2,0:T(8,128)} copy(f32[32,8,64,128]{3,2,1,0:T(8,128)S(1)} %bitcast.150) | data formatting | bytes 16777216
  193.8 9.0 %copy.61 = f32[8192,256]{1,0:T(8,128)} copy(f32[8192,256]{0,1:T(8,128)} %bitcast.152) | data formatting | bytes 16777216 | tf_op jit(solution)/shard_map/while/body/eval_jaxpr/mul | solution.py:88
  202.8 44.7 %scatter_custom_fusion.1 = f32[384,256]{1,0:T(8,128)S(1)} fusion(s32[8192]{0:T(1024)S(1)} %bitcast.169, f32[8192,256]{1,0:T(8,128)} %copy.61, f32[]{:T(128)} %constant.16.clone.1), kind=kCustom, calls=%fused_computation.51 | custom fusion | flops 2097152 | bytes 393728 | tf_op jit(solution)/shard_map/while/body/eval_jaxpr/scatter-add | solution.py:92
  247.6 0.2 bitcast_convert_fusion
  247.8 1.2 multiply_multiply_fusion
  249.1 10.9 %copy.119 = f32[32,8,64,128]{3,1,2,0:T(8,128)} copy(f32[32,8,64,128]{3,2,1,0:T(8,128)S(1)} %bitcast.151) | data formatting | bytes 16777216
  259.9 9.0 %copy.60 = f32[8192,256]{1,0:T(8,128)} copy(f32[8192,256]{0,1:T(8,128)} %bitcast.153) | data formatting | bytes 16777216 | tf_op jit(solution)/shard_map/while/body/eval_jaxpr/mul | solution.py:83
  268.9 44.9 %scatter_custom_fusion = f32[384,256]{1,0:T(8,128)S(1)} fusion(s32[8192]{0:T(1024)S(1)} %bitcast.170, f32[8192,256]{1,0:T(8,128)} %copy.60, f32[]{:T(128)} %constant.16.clone.1), kind=kCustom, calls=%fused_computation.53 | custom fusion | flops 2097152 | bytes 393728 | tf_op jit(solution)/shard_map/while/body/eval_jaxpr/scatter-add | solution.py:91
  313.9 4.0 multiply_reduce_fusion
  318.2 0.7 pad_maximum_fusion.2
  318.9 3.4 all-to-all-start.1
  322.4 0.2 fusion.11
  322.6 0.2 fusion.14
  322.8 6.4 %all-to-all-done.1 = bf16[2,8,32,256]{3,2,0,1:T(8,128)(2,1)S(1)} async-done(((bf16[2,8,32,256]{3,2,0,1:T(8,128)(2,1)}), bf16[2,8,32,256]{3,2,0,1:T(8,128)(2,1)S(1)}, u32[]{:S(2)}, u32[]{:S(2)}) %all-to-all-start.1) | async-done | bytes 262176 | tf_op jit(solution)/shard_map/all_to_all | solution.py:171
  329.3 0.4 copy.66
  329.7 8.9 %scatter_fusion = f32[2,128,256]{2,0,1:T(2,128)S(1)} fusion(f32[2,128,256]{2,0,1:T(2,128)S(1)} %copy.65, s32[256]{0:T(256)S(1)} %bitcast.172, f32[256,2,256]{2,1,0:T(2,128)S(1)} %copy.66), kind=kCustom, calls=%fused_computation.5 | custom fusion | flops 131072 | bytes 1573888 | tf_op jit(solution)/shard_map/scatter-add | solution.py:177
  339.4 0.4 copy.93
  339.8 0.9 copy.107
  340.7 108.5 %reduce-scatter.4.cloned.1.call-done = bf16[8,1024]{1,0:T(8,128)(2,1)} async-done(((bf16[256,1024]{1,0:T(8,128)(2,1)}), bf16[8,1024]{1,0:T(8,128)(2,1)}) %reduce-scatter.4.cloned.1.call-update) | async-done | bytes 16400
  449.1 0.7 reshape.281
  449.9 33.8 %psum.8 = bf16[4,8,256]{2,1,0:T(8,128)(2,1)S(1)} all-reduce(bf16[4,8,256]{2,1,0:T(8,128)(2,1)S(1)} %copy.94), channel_id=1, replica_groups=mesh['cell'=32,'brick'=8] {'brick'}, use_global_device_ids=true, to_apply=%region_8.9 | all-reduce | flops 8192 | bytes 32768 | tf_op jit(solution)/shard_map/psum | solution.py:189
  483.7 0.6 add_divide_fusion.1
  (48 shorter events, 1.7 us)
Async XLA Ops:
  7.2 1.6 copy-start
  56.4 13.4 %all-to-all-start = ((bf16[2,8,32,256]{3,2,0,1:T(8,128)(2,1)}), bf16[2,8,32,256]{3,2,0,1:T(8,128)(2,1)S(1)}, u32[]{:S(2)}, u32[]{:S(2)}) async-start(bf16[2,8,32,256]{3,2,0,1:T(8,128)(2,1)} %copy.53), calls=%async_computation | async-start | bytes 524288 | tf_op jit(solution)/shard_map/all_to_all | solution.py:150
  154.1 5.6 %copy-start.2 = (bf16[32,8,64,128]{3,2,1,0:T(8,128)(2,1)S(1)}, bf16[32,8,64,128]{3,2,1,0:T(8,128)(2,1)}, u32[]{:S(2)}) copy-start(bf16[32,8,64,128]{3,2,1,0:T(8,128)(2,1)} %copy.103) | copy-start | bytes 12582916
  154.2 6.7 %copy-start.6 = (f32[8]{0:T(128)S(1)}, f32[8]{0:T(128)}, u32[]{:S(2)}) copy-start(f32[8]{0:T(128)} %param.21) | copy-start | bytes 100
  154.2 11.8 %copy-start.5 = (f32[256]{0:T(256)S(1)}, f32[256]{0:T(256)}, u32[]{:S(2)}) copy-start(f32[256]{0:T(256)} %param.23) | copy-start | bytes 3076
  154.2 12.1 %copy-start.7 = (f32[1,1,128]{2,1,0:T(1,128)S(1)}, f32[1,1,128]{2,1,0:T(1,128)}, u32[]{:S(2)}) copy-start(f32[1,1,128]{2,1,0:T(1,128)} %param.24) | copy-start | bytes 1540
  166.3 27.5 %copy-start.8 = (f32[128]{0:T(128)}, f32[128]{0:T(128)S(1)}, u32[]{:S(2)}) copy-start(f32[128]{0:T(128)S(1)} %get-tuple-element.78) | copy-start | bytes 1540
  313.9 170.5 %copy-start.1 = (bf16[4,256]{1,0:T(4,128)(2,1)S(1)}, bf16[4,256]{1,0:T(4,128)(2,1)}, u32[]{:S(2)}) copy-start(bf16[4,256]{1,0:T(4,128)(2,1)} %param.16) | copy-start | bytes 6148
  313.9 169.8 %copy-start.3 = (f32[4,8,256]{2,1,0:T(8,128)S(1)}, f32[4,8,256]{2,1,0:T(8,128)}, u32[]{:S(2)}) copy-start(f32[4,8,256]{2,1,0:T(8,128)} %param.27) | copy-start | bytes 98308
  313.9 169.8 %copy-start.4 = (f32[4,8,256]{2,1,0:T(8,128)S(1)}, f32[4,8,256]{2,1,0:T(8,128)}, u32[]{:S(2)}) copy-start(f32[4,8,256]{2,1,0:T(8,128)} %param.26) | copy-start | bytes 98308
  318.9 10.3 %all-to-all-start.1 = ((bf16[2,8,32,256]{3,2,0,1:T(8,128)(2,1)}), bf16[2,8,32,256]{3,2,0,1:T(8,128)(2,1)S(1)}, u32[]{:S(2)}, u32[]{:S(2)}) async-start(bf16[2,8,32,256]{3,2,0,1:T(8,128)(2,1)} %pad_maximum_fusion.2), calls=%async_computation.1 | async-start | bytes 524288 | tf_op jit(solution)/shard_map/all_to_all | solution.py:171
  322.3 126.8 %reduce-scatter.4.cloned.1.call-start = ((), (), s32[]{:S(2)}) async-start(), calls=%async_computation.3 | async-start | bytes 540672
Sparse Core Ops, SparseCore 0:
  340.8 108.2 reduce-scatter.3
where the time goes:
time: 496 us; the launch traced here: 491 us
  local copies, waits for them, and re-layouts  147 us (30%)
  other arithmetic  120 us (24%)
  waiting for transfers between devices  120 us (24%)
  blocking collectives  77.2 us (16%)
  between operations  14.7 us (3%)
  starting transfers between devices  9.37 us (2%)
    unnamed x2, waiting for transfers between devices  108 us
    unnamed x26, local copies, waits for them, and re-layouts  46.4 us
    scatter-add x1, other arithmetic, tile_step(): key_grads.at[flattened_rows].add(key_edge.reshape(-1, model_width))  44.9 us
    scatter-add x1, other arithmetic, tile_step(): value_grads.at[flattened_rows].add(value_edge.reshape(-1, model_width))  44.7 us
    all_gather x1, blocking collectives, body(): lax.all_gather(master.astype(jnp.bfloat16), 'cell', axis=1, tiled=True)  43.4 us
    gather x2, local copies, waits for them, and re-layouts, tile_step(): value_table[neighbour_rows].reshape(slot_count, TILE, head_count, head_size)  39.7 us
    gather x2, local copies, waits for them, and re-layouts, tile_step(): key_table[neighbour_rows].reshape(slot_count, TILE, head_count, head_size)  39.3 us
    psum x1, blocking collectives, body(): summed = lax.psum(grads.astype(jnp.bfloat16), 'brick')  33.8 us
  transfers between devices with their start and end apart: 3, of which 3 were waited for; matrix products, arithmetic and copies ran while one was open for 1% of the time, Pallas kernels for 0%

commit v1 on v0

--- a/solution.py
+++ b/solution.py
@@ -1,3 +1,4 @@
+import functools
 import math
 import jax
 import jax.numpy as jnp
@@ -7,6 +8,13 @@
 TILE = 128
 loss_weight = 0.0625
 epsilon_norm = 1e-06
+
+
+def _place_quotas(frame_in, named_axis):
+    return jnp.sum(lax.all_gather(frame_in, named_axis), 0)
+
+
+column_draft = functools.partial(_place_quotas, named_axis="brick")
 
 
 def silu_slope(inputs):
@@ -186,7 +194,7 @@
     grad_v = jnp.einsum("ac,ad->cd", normed_features, totals[1], preferred_element_type=jnp.float32)
     grad_o = jnp.einsum("ac,ad->cd", attended, grad_updated, preferred_element_type=jnp.float32)
     grads = jnp.stack([grad_q, key_gradient, grad_v, grad_o])
-    summed = lax.psum(grads.astype(jnp.bfloat16), "brick")
+    summed = column_draft(grads.astype(jnp.bfloat16))
     owned = lax.psum_scatter(summed, "cell", scatter_dimension=1, tiled=True).astype(jnp.float32)
     moment_new = 0.9 * moment + 0.1 * owned
     second_new = 0.999 * second + 0.001 * owned * owned

time: 496 us -> 561 us (1.13)
  waiting for transfers between devices: 120 us -> 213 us
  blocking collectives: 77.2 us -> 43.4 us
    all_gather x0 -> x1, waiting for transfers between devices: none -> 86.7 us  [_place_quotas(): return jnp.sum(lax.all_gather(frame_in, named_axis), 0)]
    psum x1 -> x0, blocking collectives: 33.8 us -> none  [body(): summed = lax.psum(grads.astype(jnp.bfloat16), 'brick')]
    unnamed x2 -> x3, waiting for transfers between devices: 108 us -> 115 us
    unnamed x26 -> x25, local copies, waits for them, and re-layouts: 46.4 us -> 46.4 us
  transfers between devices with their start and end apart: 3 -> 4, of which waited for: 3 -> 4; matrix products, arithmetic and copies ran while one was open for 1% -> 1% of each run, Pallas kernels for 0% -> 0%
where the time goes in v1:
time: 561 us; the launch traced here: 555 us
  waiting for transfers between devices  213 us (38%)
  local copies, waits for them, and re-layouts  147 us (26%)
  other arithmetic  124 us (22%)
  blocking collectives  43.4 us (8%)
  between operations  14.7 us (3%)
  starting transfers between devices  9.41 us (2%)
    unnamed x3, waiting for transfers between devices  115 us
    all_gather x1, waiting for transfers between devices, _place_quotas(): return jnp.sum(lax.all_gather(frame_in, named_axis), 0)  86.7 us
    unnamed x25, local copies, waits for them, and re-layouts  46.4 us
    scatter-add x1, other arithmetic, tile_step(): key_grads.at[flattened_rows].add(key_edge.reshape(-1, model_width))  44.9 us
    scatter-add x1, other arithmetic, tile_step(): value_grads.at[flattened_rows].add(value_edge.reshape(-1, model_width))  44.7 us
    all_gather x1, blocking collectives, body(): lax.all_gather(master.astype(jnp.bfloat16), 'cell', axis=1, tiled=True)  43.4 us
    gather x2, local copies, waits for them, and re-layouts, tile_step(): value_table[neighbour_rows].reshape(slot_count, TILE, head_count, head_size)  39.7 us
    gather x2, local copies, waits for them, and re-layouts, tile_step(): key_table[neighbour_rows].reshape(slot_count, TILE, head_count, head_size)  39.3 us
  transfers between devices with their start and end apart: 4, of which 4 were waited for; matrix products, arithmetic and copies ran while one was open for 1% of the time, Pallas kernels for 0%

profile of v1, /device:TPU:16, one launch (start us, length us, event | category | flops | bytes accessed | tf_op | source)
XLA Modules:
  0.0 554.5 jit_solution(18028913034369532969)
XLA Ops:
  7.2 0.8 reshape_squeeze.17
  8.0 0.8 convert_element_type.88
  8.7 1.2 multiply_reduce_fusion.5
  9.9 43.4 %all_gather.7 = bf16[4,256,256]{2,1,0:T(8,128)(2,1)S(1)} all-gather(bf16[4,8,256]{2,1,0:T(8,128)(2,1)S(1)} %convert_element_type.88), channel_id=1, replica_groups=mesh['cell'=32,'brick'=8] {'cell'}, dimensions={1}, use_global_device_ids=true | all-gather | bytes 540672 | tf_op jit(solution)/shard_map/all_gather | solution.py:152
  53.3 0.8 multiply_convert_fusion.2
  54.1 0.2 fusion.10
  54.5 1.2 gather_fusion
  55.7 0.7 copy.53
  56.4 5.9 %all-to-all-start = ((bf16[2,8,32,256]{3,2,0,1:T(8,128)(2,1)}), bf16[2,8,32,256]{3,2,0,1:T(8,128)(2,1)S(1)}, u32[]{:S(2)}, u32[]{:S(2)}) async-start(bf16[2,8,32,256]{3,2,0,1:T(8,128)(2,1)} %copy.53), calls=%async_computation | async-start | bytes 524288 | tf_op jit(solution)/shard_map/all_to_all | solution.py:158
  62.4 0.8 compare_select_fusion
  63.2 0.7 iota_compare_fusion.2
  64.0 0.8 fusion.37
  64.8 5.0 all-to-all-done
  69.9 32.9 %gather_fusion.1 = bf16[8192,256]{1,0:T(8,128)(2,1)} fusion(bf16[384,256]{1,0:T(8,128)(2,1)S(1)} %get-tuple-element.81, s32[8192]{0:T(1024)S(1)} %fusion.37), kind=kCustom, calls=%fused_computation.1 | custom fusion | bytes 8421376 | tf_op jit(solution)/shard_map/while/body/eval_jaxpr/gather | solution.py:52
  102.8 6.4 %copy.55 = bf16[8192,256]{0,1:T(8,128)(2,1)} copy(bf16[8192,256]{1,0:T(8,128)(2,1)} %gather_fusion.1) | data formatting | bytes 8388608 | tf_op jit(solution)/shard_map/while/body/eval_jaxpr/gather | solution.py:52
  109.2 5.3 copy.103
  114.5 32.9 %gather_fusion.2 = bf16[8192,256]{1,0:T(8,128)(2,1)} fusion(bf16[384,256]{1,0:T(8,128)(2,1)S(1)} %get-tuple-element.82, s32[8192]{0:T(1024)S(1)} %fusion.37), kind=kCustom, calls=%fused_computation.2 | custom fusion | bytes 8421376 | tf_op jit(solution)/shard_map/while/body/eval_jaxpr/gather | solution.py:53
  147.4 6.7 %copy.58 = bf16[8192,256]{0,1:T(8,128)(2,1)} copy(bf16[8192,256]{1,0:T(8,128)(2,1)} %gather_fusion.2) | data formatting | bytes 8388608 | tf_op jit(solution)/shard_map/while/body/eval_jaxpr/gather | solution.py:53
  154.2 5.5 copy.104
  159.7 1.2 multiply_reduce_fusion.3
  160.9 1.1 convert_convert_fusion
  162.0 4.0 multiply_reduce_fusion.2
  166.0 0.3 multiply_reduce_fusion.4
  166.7 3.4 multiply_reduce_fusion.1
  170.1 1.1 broadcast_multiply_fusion
  171.2 22.6 %copy.122 = f32[32,8,64,128]{3,1,2,0:T(8,128)} copy(f32[32,8,64,128]{3,2,1,0:T(8,128)S(1)} %bitcast.150) | data formatting | bytes 16777216
  193.8 9.0 %copy.61 = f32[8192,256]{1,0:T(8,128)} copy(f32[8192,256]{0,1:T(8,128)} %bitcast.152) | data formatting | bytes 16777216 | tf_op jit(solution)/shard_map/while/body/eval_jaxpr/mul | solution.py:96
  202.8 44.7 %scatter_custom_fusion.1 = f32[384,256]{1,0:T(8,128)S(1)} fusion(s32[8192]{0:T(1024)S(1)} %bitcast.169, f32[8192,256]{1,0:T(8,128)} %copy.61, f32[]{:T(128)} %constant.17.clone.1), kind=kCustom, calls=%fused_computation.51 | custom fusion | flops 2097152 | bytes 393728 | tf_op jit(solution)/shard_map/while/body/eval_jaxpr/scatter-add | solution.py:100
  247.6 0.2 bitcast_convert_fusion
  247.8 1.2 multiply_multiply_fusion
  249.1 10.9 %copy.123 = f32[32,8,64,128]{3,1,2,0:T(8,128)} copy(f32[32,8,64,128]{3,2,1,0:T(8,128)S(1)} %bitcast.151) | data formatting | bytes 16777216
  259.9 9.0 %copy.60 = f32[8192,256]{1,0:T(8,128)} copy(f32[8192,256]{0,1:T(8,128)} %bitcast.153) | data formatting | bytes 16777216 | tf_op jit(solution)/shard_map/while/body/eval_jaxpr/mul | solution.py:91
  268.9 44.9 %scatter_custom_fusion = f32[384,256]{1,0:T(8,128)S(1)} fusion(s32[8192]{0:T(1024)S(1)} %bitcast.170, f32[8192,256]{1,0:T(8,128)} %copy.60, f32[]{:T(128)} %constant.17.clone.1), kind=kCustom, calls=%fused_computation.53 | custom fusion | flops 2097152 | bytes 393728 | tf_op jit(solution)/shard_map/while/body/eval_jaxpr/scatter-add | solution.py:99
  313.9 4.0 multiply_reduce_fusion
  318.2 0.7 pad_maximum_fusion.2
  318.9 3.4 all-to-all-start.1
  322.6 0.2 fusion.14
  322.8 6.4 %all-to-all-done.1 = bf16[2,8,32,256]{3,2,0,1:T(8,128)(2,1)S(1)} async-done(((bf16[2,8,32,256]{3,2,0,1:T(8,128)(2,1)}), bf16[2,8,32,256]{3,2,0,1:T(8,128)(2,1)S(1)}, u32[]{:S(2)}, u32[]{:S(2)}) %all-to-all-start.1) | async-done | bytes 262176 | tf_op jit(solution)/shard_map/all_to_all | solution.py:179
  329.3 0.4 copy.66
  329.7 8.9 %scatter_fusion = f32[2,128,256]{2,0,1:T(2,128)S(1)} fusion(f32[2,128,256]{2,0,1:T(2,128)S(1)} %copy.65, s32[256]{0:T(256)S(1)} %bitcast.172, f32[256,2,256]{2,1,0:T(2,128)S(1)} %copy.66), kind=kCustom, calls=%fused_computation.5 | custom fusion | flops 131072 | bytes 1573888 | tf_op jit(solution)/shard_map/scatter-add | solution.py:185
  339.3 0.9 pad_maximum_fusion
  340.2 86.7 %all-gather.2.cloned.1.call-done = bf16[8,4,256,256]{3,2,1,0:T(8,128)(2,1)} async-done(((bf16[1,4,256,256]{3,2,1,0:T(8,128)(2,1)}), bf16[8,4,256,256]{3,2,1,0:T(8,128)(2,1)}) %all-gather.2.cloned.1.call-update) | async-done | bytes 4194320 | tf_op jit(solution)/shard_map/all_gather | solution.py:14
  426.9 2.8 reduce_sum.55
  429.8 0.4 copy.93
  430.2 0.9 copy.107
  431.1 115.0 %reduce-scatter.4.cloned.1.call-done = bf16[8,1024]{1,0:T(8,128)(2,1)} async-done(((bf16[256,1024]{1,0:T(8,128)(2,1)}), bf16[8,1024]{1,0:T(8,128)(2,1)}) %reduce-scatter.4.cloned.1.call-update) | async-done | bytes 16400
  546.1 0.7 reshape.344
  546.8 0.6 add_divide_fusion.1
  (50 shorter events, 2.1 us)
Async XLA Ops:
  7.2 1.6 copy-start
  56.4 13.4 %all-to-all-start = ((bf16[2,8,32,256]{3,2,0,1:T(8,128)(2,1)}), bf16[2,8,32,256]{3,2,0,1:T(8,128)(2,1)S(1)}, u32[]{:S(2)}, u32[]{:S(2)}) async-start(bf16[2,8,32,256]{3,2,0,1:T(8,128)(2,1)} %copy.53), calls=%async_computation | async-start | bytes 524288 | tf_op jit(solution)/shard_map/all_to_all | solution.py:158
  154.1 5.6 %copy-start.2 = (bf16[32,8,64,128]{3,2,1,0:T(8,128)(2,1)S(1)}, bf16[32,8,64,128]{3,2,1,0:T(8,128)(2,1)}, u32[]{:S(2)}) copy-start(bf16[32,8,64,128]{3,2,1,0:T(8,128)(2,1)} %copy.103) | copy-start | bytes 12582916
  154.2 6.7 %copy-start.6 = (f32[8]{0:T(128)S(1)}, f32[8]{0:T(128)}, u32[]{:S(2)}) copy-start(f32[8]{0:T(128)} %param.21) | copy-start | bytes 100
  154.2 11.8 %copy-start.5 = (f32[256]{0:T(256)S(1)}, f32[256]{0:T(256)}, u32[]{:S(2)}) copy-start(f32[256]{0:T(256)} %param.23) | copy-start | bytes 3076
  154.2 12.1 %copy-start.7 = (f32[1,1,128]{2,1,0:T(1,128)S(1)}, f32[1,1,128]{2,1,0:T(1,128)}, u32[]{:S(2)}) copy-start(f32[1,1,128]{2,1,0:T(1,128)} %param.24) | copy-start | bytes 1540
  166.3 27.5 %copy-start.8 = (f32[128]{0:T(128)}, f32[128]{0:T(128)S(1)}, u32[]{:S(2)}) copy-start(f32[128]{0:T(128)S(1)} %get-tuple-element.78) | copy-start | bytes 1540
  317.9 228.9 %copy-start.3 = (f32[4,8,256]{2,1,0:T(8,128)S(1)}, f32[4,8,256]{2,1,0:T(8,128)}, u32[]{:S(2)}) copy-start(f32[4,8,256]{2,1,0:T(8,128)} %param.27) | copy-start | bytes 98308
  317.9 228.9 %copy-start.4 = (f32[4,8,256]{2,1,0:T(8,128)S(1)}, f32[4,8,256]{2,1,0:T(8,128)}, u32[]{:S(2)}) copy-start(f32[4,8,256]{2,1,0:T(8,128)} %param.26) | copy-start | bytes 98308
  317.9 229.5 %copy-start.1 = (bf16[4,256]{1,0:T(4,128)(2,1)S(1)}, bf16[4,256]{1,0:T(4,128)(2,1)}, u32[]{:S(2)}) copy-start(bf16[4,256]{1,0:T(4,128)(2,1)} %param.16) | copy-start | bytes 6148
  318.9 10.3 %all-to-all-start.1 = ((bf16[2,8,32,256]{3,2,0,1:T(8,128)(2,1)}), bf16[2,8,32,256]{3,2,0,1:T(8,128)(2,1)S(1)}, u32[]{:S(2)}, u32[]{:S(2)}) async-start(bf16[2,8,32,256]{3,2,0,1:T(8,128)(2,1)} %pad_maximum_fusion.2), calls=%async_computation.1 | async-start | bytes 524288 | tf_op jit(solution)/shard_map/all_to_all | solution.py:179
  322.3 104.6 %all-gather.2.cloned.1.call-start = ((), (), s32[]{:S(2)}) async-start(), calls=%async_computation.3 | async-start | bytes 4718592 | tf_op jit(solution)/shard_map/all_gather | solution.py:14
  340.2 205.9 %reduce-scatter.4.cloned.1.call-start = ((), (), s32[]{:S(2)}) async-start(), calls=%async_computation.4 | async-start | bytes 540672
Sparse Core Ops, SparseCore 0:
  340.3 86.5 all-gather.1
  431.2 114.8 reduce-scatter.3
